TPU v7x, 512 devices: a whole 4x4x16 slice. The times are simulated.
512 devices in a mesh: hid: 64 (over y, x, z_hi, core), mod: 8 (over z_lo).
Axes of the slice: x: 4, y: 4, z: 16 (z_hi: 2, z_lo: 8; z = z_hi * 8 + z_lo), core: 2. Of those that a mesh axis runs over, the one named last changes fastest.
Arguments:
- tokens: bfloat16 [512, 8192], P('hid', 'mod'), may hold values from -6 to 6
- cotangent: bfloat16 [512, 8192], P('hid', 'mod'), may hold values from -1.2578125 to 1.2578125
- gate_weight: bfloat16 [8192, 26624], P('mod', 'hid'), may hold values from -0.0625 to 0.0625
- up_weight: bfloat16 [8192, 26624], P('mod', 'hid'), may hold values from -0.0625 to 0.0625
- down_weight: bfloat16 [26624, 8192], P('hid', 'mod'), may hold values from -0.0390625 to 0.0390625
Outputs:
- grad_in: bfloat16 [512, 8192], P('hid', 'mod')
- grad_gate: bfloat16 [8192, 26624], P('mod', 'hid')
- grad_up: bfloat16 [8192, 26624], P('mod', 'hid')
- grad_down: bfloat16 [26624, 8192], P('hid', 'mod')
All inputs are finite; a program needn't handle non-finite values.
Results may differ from a plain program's by a relative error of at most 0.027.
Values may be sent and summed in bfloat16 or wider, within the bound.
A program may use at most 64 MiB of HBM per device.

v0:
```python
import jax
import jax.numpy as jnp
from jax import lax
from jax.sharding import PartitionSpec as P

readout_scale = 2.0


def contract_last(left, right):
    return lax.dot_general(
        left, right, (((1,), (1,)), ((), ())), preferred_element_type=jnp.float32
    )


def contract_first(left, right):
    return lax.dot_general(
        left, right, (((0,), (0,)), ((), ())), preferred_element_type=jnp.float32
    )


def swiglu_grads(gate, up, back):
    back = readout_scale * back
    sigmoid_gate = jax.nn.sigmoid(gate)
    activated = gate * sigmoid_gate
    hidden = (activated * up).astype(jnp.bfloat16)
    d_gate = (back * up * sigmoid_gate * (1.0 + gate * (1.0 - sigmoid_gate))).astype(jnp.bfloat16)
    d_up = (back * activated).astype(jnp.bfloat16)
    return (hidden, d_gate, d_up)


def local(tokens, cotangent, gate_weight, up_weight, down_weight):
    piece = lax.all_gather(tokens, "hid", axis=0, tiled=True)
    token_rows = piece
    gate_part = jnp.dot(piece, gate_weight, preferred_element_type=jnp.float32)
    up_part = jnp.dot(piece, up_weight, preferred_element_type=jnp.float32)
    piece = lax.all_gather(cotangent, "hid", axis=0, tiled=True)
    back_part = contract_last(piece, down_weight)
    gate_sum, up_sum, back_sum = (
        lax.psum(gate_part.astype(jnp.bfloat16), "mod").astype(jnp.float32),
        lax.psum(up_part.astype(jnp.bfloat16), "mod").astype(jnp.float32),
        lax.psum(back_part.astype(jnp.bfloat16), "mod").astype(jnp.float32),
    )
    hidden, d_gate, d_up = swiglu_grads(gate_sum, up_sum, back_sum)
    grad_down = (readout_scale * contract_first(hidden, piece)).astype(jnp.bfloat16)
    grad_gate = contract_first(token_rows, d_gate).astype(jnp.bfloat16)
    grad_up = contract_first(token_rows, d_up).astype(jnp.bfloat16)
    grad_in = lax.psum_scatter(
        contract_last(d_gate, gate_weight) + contract_last(d_up, up_weight),
        "hid",
        scatter_dimension=0,
        tiled=True,
    ).astype(jnp.bfloat16)
    return (grad_in, grad_gate, grad_up, grad_down)


def solution(mesh):
    placed = (P("hid", "mod"), P("hid", "mod"), P("mod", "hid"), P("mod", "hid"), P("hid", "mod"))
    return jax.shard_map(
        local,
        mesh=mesh,
        in_specs=placed,
        out_specs=(P("hid", "mod"), P("mod", "hid"), P("mod", "hid"), P("hid", "mod")),
        check_vma=False,
    )
```

profile of v0, /device:TPU:32, one launch (start us, length us, event | category | flops | bytes accessed | tf_op | source)
XLA Modules:
  0.0 922.5 jit_solution(11970317265629496496)
XLA Ops:
  7.2 0.0 copy-start
  7.2 0.0 all-gather.5.cloned.1.call-start
  7.2 0.7 all-gather.5.cloned.1.call-update
  7.9 0.0 all-gather.3.cloned.1.call-start
  8.0 0.7 all-gather.3.cloned.1.call-update
  8.7 0.0 all-reduce.3.cloned.1.call-start
  8.7 104.6 %all-gather.5.cloned.1.call-done = bf16[512,1024]{1,0:T(8,128)(2,1)} async-done(((bf16[8,1024]{1,0:T(8,128)(2,1)}), bf16[512,1024]{1,0:T(8,128)(2,1)}) %all-gather.5.cloned.1.call-update) | async-done | bytes 1048592 | tf_op jit(solution)/shard_map/all_gather | solution.py:32
  113.3 2.8 convolution_convert_fusion.2
  116.1 0.0 copy-done.4
  116.1 1.4 convolution_convert_fusion.3
  117.5 92.6 %all-gather.3.cloned.1.call-done = bf16[512,1024]{1,0:T(8,128)(2,1)} async-done(((bf16[8,1024]{1,0:T(8,128)(2,1)}), bf16[512,1024]{1,0:T(8,128)(2,1)}) %all-gather.3.cloned.1.call-update) | async-done | bytes 1048592 | tf_op jit(solution)/shard_map/all_gather | solution.py:36
  210.1 2.6 convolution_convert_fusion.4
  212.7 0.0 all-reduce.3.cloned.1.call-update
  212.7 0.0 reduce-scatter.2.cloned.1.call-start
  212.8 121.7 %all-reduce.3.cloned.1.call-done = (bf16[512,416]{0,1:T(8,128)(2,1)}, bf16[512,416]{0,1:T(8,128)(2,1)}, bf16[512,416]{0,1:T(8,128)(2,1)}) async-done(((bf16[512,416]{0,1:T(8,128)(2,1)}, bf16[512,416]{0,1:T(8,128)(2,1)}, bf16[512,416]{0,1:T(8,128)(2,1)}), (bf16[512,416]{0,1:T(8,128)(2,1)}, bf16[512,416]{0,1:T(8,128)(2,1)}, bf16[512,416]{0,1:T(8,128)(2,1)})) %all-reduce.3.cloned.1.call-update) | async-done | bytes 1277968 | tf_op jit(solution)/shard_map/psum | solution.py:40
  334.5 2.3 fusion.13
  336.9 2.2 convolution_add_fusion
  339.1 0.0 reduce-scatter.2.cloned.1.call-update
  339.1 0.0 copy-start.2
  339.1 1.6 fusion.1
  340.7 1.6 multiply_convert_fusion
  342.3 1.7 fusion
  344.0 570.5 %reduce-scatter.2.cloned.1.call-done = f32[8,1024]{1,0:T(8,128)} async-done(((f32[512,1024]{1,0:T(8,128)}), f32[8,1024]{1,0:T(8,128)}) %reduce-scatter.2.cloned.1.call-update) | async-done | bytes 32784 | tf_op jit(solution)/shard_map/reduce_scatter | solution.py:47
  914.6 1.4 convert_element_type.53
  (15 shorter events, 0.0 us)
Async XLA Ops:
  7.2 106.1 %copy-start = (bf16[1024,416]{0,1:T(8,128)(2,1)S(1)}, bf16[1024,416]{0,1:T(8,128)(2,1)}, u32[]{:S(2)}) copy-start(bf16[1024,416]{0,1:T(8,128)(2,1)} %param.7) | copy-start | bytes 2555908
  7.2 106.1 %all-gather.5.cloned.1.call-start = ((), (), s32[]{:S(2)}) async-start(), calls=%async_computation.2 | async-start | bytes 1064960 | tf_op jit(solution)/shard_map/all_gather | solution.py:32
  7.9 202.2 %all-gather.3.cloned.1.call-start = ((), (), s32[]{:S(2)}) async-start(), calls=%async_computation.1 | async-start | bytes 1064960 | tf_op jit(solution)/shard_map/all_gather | solution.py:36
  8.7 325.9 %all-reduce.3.cloned.1.call-start = ((), (), s32[]{:S(2)}) async-start(), calls=%async_computation.4 | async-start | bytes 2555904 | tf_op jit(solution)/shard_map/psum | solution.py:40
  113.3 2.8 copy-start.1
  113.3 2.8 copy-start.4
  116.1 94.0 %copy-start.3 = (bf16[416,1024]{1,0:T(8,128)(2,1)S(1)}, bf16[416,1024]{1,0:T(8,128)(2,1)}, u32[]{:S(2)}) copy-start(bf16[416,1024]{1,0:T(8,128)(2,1)} %param.9) | copy-start | bytes 2555908
  212.7 701.8 %reduce-scatter.2.cloned.1.call-start = ((), (), s32[]{:S(2)}) async-start(), calls=%async_computation.3 | async-start | bytes 2129920 | tf_op jit(solution)/shard_map/reduce_scatter | solution.py:47
  334.5 2.3 copy-start.5
  334.5 2.4 copy-start.7
  334.5 2.4 copy-start.8
  339.1 1.6 copy-start.2
  339.1 1.6 copy-start.6
Sparse Core Ops, SparseCore 0:
  12.4 100.8 all-gather.4
  117.6 92.4 all-gather.2
  213.8 120.6 all-reduce.2
  339.2 575.2 reduce-scatter.1
where the time goes:
time: 923 us; the launch traced here: 922 us
  waiting for transfers between devices  891 us (97%)
  matrix products  16.2 us (2%)
  between operations  13.8 us (1%)
    reduce_scatter x1, waiting for transfers between devices, local(): lax.psum_scatter(contract_last(d_gate, gate_weight) + contract_last(d_up,...  571 us
    psum x1, waiting for transfers between devices, local(): lax.psum(up_part.astype(jnp.bfloat16), 'mod').astype(jnp.float32)  122 us
    all_gather x1, waiting for transfers between devices, local(): piece = lax.all_gather(tokens, 'hid', axis=0, tiled=True)  105 us
    all_gather x1, waiting for transfers between devices, local(): piece = lax.all_gather(cotangent, 'hid', axis=0, tiled=True)  92.6 us
  transfers between devices with their start and end apart: 4, of which 4 were waited for; matrix products, arithmetic and copies ran while one was open for 1% of the time, Pallas kernels for 0%

commit v1 on v0

--- a/solution.py
+++ b/solution.py
@@ -29,7 +29,8 @@
 
 
 def local(tokens, cotangent, gate_weight, up_weight, down_weight):
-    piece = lax.all_gather(tokens, "hid", axis=0, tiled=True)
+    mid_arr = jax.lax.all_to_all(jnp.stack([tokens] * jax.lax.axis_size("hid"), 0), "hid", 0, 0)
+    piece = jnp.concatenate(mid_arr, 0)
     token_rows = piece
     gate_part = jnp.dot(piece, gate_weight, preferred_element_type=jnp.float32)
     up_part = jnp.dot(piece, up_weight, preferred_element_type=jnp.float32)

time: 923 us -> 865 us (0.937)
  waiting for transfers between devices: 891 us -> 811 us
  starting transfers between devices: 0.16 us -> 20.4 us
    all_gather x1 -> x0, waiting for transfers between devices: 105 us -> none  [local(): piece = lax.all_gather(tokens, 'hid', axis=0, tiled=True)]
    all_gather x1, waiting for transfers between devices: 92.6 us -> 118 us  [local(): piece = lax.all_gather(cotangent, 'hid', axis=0, tiled=True)]
    all_to_all x0 -> x1, starting transfers between devices: none -> 20.3 us  [local(): jax.lax.all_to_all(jnp.stack([tokens] * jax.lax.axis_size('hid'), 0), 'hi...]
  transfers between devices with their start and end apart: 4 -> 4, of which waited for: 4 -> 3; matrix products, arithmetic and copies ran while one was open for 1% -> 1% of each run, Pallas kernels for 0% -> 0%
where the time goes in v1:
time: 865 us; the launch traced here: 864 us
  waiting for transfers between devices  811 us (94%)
  starting transfers between devices  20.4 us (2%)
  matrix products  16 us (2%)
  between operations  13.8 us (2%)
    reduce_scatter x1, waiting for transfers between devices, local(): lax.psum_scatter(contract_last(d_gate, gate_weight) + contract_last(d_up,...  571 us
    psum x1, waiting for transfers between devices, local(): lax.psum(up_part.astype(jnp.bfloat16), 'mod').astype(jnp.float32)  120 us
    all_gather x1, waiting for transfers between devices, local(): piece = lax.all_gather(cotangent, 'hid', axis=0, tiled=True)  118 us
    all_to_all x1, starting transfers between devices, local(): jax.lax.all_to_all(jnp.stack([tokens] * jax.lax.axis_size('hid'), 0), 'hi...  20.3 us
  transfers between devices with their start and end apart: 4, of which 3 were waited for; matrix products, arithmetic and copies ran while one was open for 1% of the time, Pallas kernels for 0%

profile of v1, /device:TPU:32, one launch (start us, length us, event | category | flops | bytes accessed | tf_op | source)
XLA Modules:
  0.0 864.2 jit_solution(8224992569209504013)
XLA Ops:
  7.2 0.0 copy-start
  7.2 1.9 stack.2
  9.1 20.3 %all-to-all-start = ((bf16[64,8,1024]{2,1,0:T(8,128)(2,1)}), bf16[64,8,1024]{2,1,0:T(8,128)(2,1)S(1)}, u32[]{:S(2)}, u32[]{:S(2)}) async-start(bf16[64,8,1024]{2,1,0:T(8,128)(2,1)} %stack.2), calls=%async_computation | async-start | bytes 2097152 | tf_op jit(solution)/shard_map/all_to_all | solution.py:32
  29.4 0.0 all-gather.2.cloned.1.call-start
  29.5 0.7 all-gather.2.cloned.1.call-update
  30.2 0.0 all-reduce.3.cloned.1.call-start
  30.2 118.3 %all-gather.2.cloned.1.call-done = bf16[512,1024]{1,0:T(8,128)(2,1)} async-done(((bf16[8,1024]{1,0:T(8,128)(2,1)}), bf16[512,1024]{1,0:T(8,128)(2,1)}) %all-gather.2.cloned.1.call-update) | async-done | bytes 1048592 | tf_op jit(solution)/shard_map/all_gather | solution.py:37
  148.5 2.6 convolution_convert_fusion.4
  151.1 0.0 all-to-all-done
  151.1 2.6 convolution_convert_fusion.3
  153.7 1.4 convolution_convert_fusion.2
  155.1 0.0 all-reduce.3.cloned.1.call-update
  155.1 0.0 reduce-scatter.2.cloned.1.call-start
  155.2 120.4 %all-reduce.3.cloned.1.call-done = (bf16[512,416]{0,1:T(8,128)(2,1)}, bf16[512,416]{0,1:T(8,128)(2,1)}, bf16[512,416]{0,1:T(8,128)(2,1)}) async-done(((bf16[512,416]{0,1:T(8,128)(2,1)}, bf16[512,416]{0,1:T(8,128)(2,1)}, bf16[512,416]{0,1:T(8,128)(2,1)}), (bf16[512,416]{0,1:T(8,128)(2,1)}, bf16[512,416]{0,1:T(8,128)(2,1)}, bf16[512,416]{0,1:T(8,128)(2,1)})) %all-reduce.3.cloned.1.call-update) | async-done | bytes 1277968 | tf_op jit(solution)/shard_map/psum | solution.py:41
  275.6 2.3 fusion.17
  278.0 2.2 convolution_add_fusion
  280.1 0.0 reduce-scatter.2.cloned.1.call-update
  280.2 0.0 copy-start.1
  280.2 0.0 copy-start.4
  280.2 1.6 fusion.1
  281.8 1.6 multiply_convert_fusion
  283.4 1.7 fusion
  285.1 571.2 %reduce-scatter.2.cloned.1.call-done = f32[8,1024]{1,0:T(8,128)} async-done(((f32[512,1024]{1,0:T(8,128)}), f32[8,1024]{1,0:T(8,128)}) %reduce-scatter.2.cloned.1.call-update) | async-done | bytes 32784 | tf_op jit(solution)/shard_map/reduce_scatter | solution.py:48
  856.4 1.4 convert_element_type.53
  (11 shorter events, 0.0 us)
Async XLA Ops:
  7.2 146.5 %copy-start = (bf16[1024,416]{0,1:T(8,128)(2,1)S(1)}, bf16[1024,416]{0,1:T(8,128)(2,1)}, u32[]{:S(2)}) copy-start(bf16[1024,416]{0,1:T(8,128)(2,1)} %param.7) | copy-start | bytes 2555908
  7.2 141.3 %copy-start.2 = (bf16[416,1024]{1,0:T(8,128)(2,1)S(1)}, bf16[416,1024]{1,0:T(8,128)(2,1)}, u32[]{:S(2)}) copy-start(bf16[416,1024]{1,0:T(8,128)(2,1)} %param.9) | copy-start | bytes 2555908
  9.1 142.0 %all-to-all-start = ((bf16[64,8,1024]{2,1,0:T(8,128)(2,1)}), bf16[64,8,1024]{2,1,0:T(8,128)(2,1)S(1)}, u32[]{:S(2)}, u32[]{:S(2)}) async-start(bf16[64,8,1024]{2,1,0:T(8,128)(2,1)} %stack.2), calls=%async_computation | async-start | bytes 2097152 | tf_op jit(solution)/shard_map/all_to_all | solution.py:32
  29.4 119.1 %all-gather.2.cloned.1.call-start = ((), (), s32[]{:S(2)}) async-start(), calls=%async_computation.2 | async-start | bytes 1064960 | tf_op jit(solution)/shard_map/all_gather | solution.py:37
  30.2 245.4 %all-reduce.3.cloned.1.call-start = ((), (), s32[]{:S(2)}) async-start(), calls=%async_computation.4 | async-start | bytes 2555904 | tf_op jit(solution)/shard_map/psum | solution.py:41
  155.1 701.2 %reduce-scatter.2.cloned.1.call-start = ((), (), s32[]{:S(2)}) async-start(), calls=%async_computation.3 | async-start | bytes 2129920 | tf_op jit(solution)/shard_map/reduce_scatter | solution.py:48
  275.6 2.3 copy-start.3
  275.6 2.4 copy-start.5
  275.6 2.4 copy-start.6
  280.2 1.6 copy-start.1
  280.2 1.6 copy-start.4
Sparse Core Ops, SparseCore 0:
  34.6 113.8 all-gather.1
  155.2 120.3 all-reduce.2
  280.3 576.0 reduce-scatter.1

commit v2 on v0

--- a/solution.py
+++ b/solution.py
@@ -4,6 +4,12 @@
 from jax.sharding import PartitionSpec as P
 
 readout_scale = 2.0
+
+
+def gather_and_add(array, name):
+    parts = lax.all_gather(array, name, axis=0, tiled=False)
+    total = parts.sum(axis=0)
+    return total
 
 
 def contract_last(left, right):
@@ -37,7 +43,7 @@
     back_part = contract_last(piece, down_weight)
     gate_sum, up_sum, back_sum = (
         lax.psum(gate_part.astype(jnp.bfloat16), "mod").astype(jnp.float32),
-        lax.psum(up_part.astype(jnp.bfloat16), "mod").astype(jnp.float32),
+        gather_and_add(up_part.astype(jnp.bfloat16), "mod").astype(jnp.float32),
         lax.psum(back_part.astype(jnp.bfloat16), "mod").astype(jnp.float32),
     )
     hidden, d_gate, d_up = swiglu_grads(gate_sum, up_sum, back_sum)

time: 923 us -> 1000 us (1.083)
  waiting for transfers between devices: 891 us -> 965 us
    all_gather x0 -> x1, waiting for transfers between devices: none -> 78.6 us  [gather_and_add(): parts = lax.all_gather(array, name, axis=0, tiled=False)]
  transfers between devices with their start and end apart: 4 -> 5, of which waited for: 4 -> 5; matrix products, arithmetic and copies ran while one was open for 1% -> 2% of each run, Pallas kernels for 0% -> 0%
where the time goes in v2:
time: 1000 us
  waiting for transfers between devices  965 us (96%)
  matrix products  16.3 us (2%)
  between operations  13.8 us (1%)
    reduce_scatter x1, waiting for transfers between devices, local(): lax.psum_scatter(contract_last(d_gate, gate_weight) + contract_last(d_up,...  571 us
    psum x1, waiting for transfers between devices, local(): lax.psum(gate_part.astype(jnp.bfloat16), 'mod').astype(jnp.float32)  117 us
    all_gather x1, waiting for transfers between devices, local(): piece = lax.all_gather(tokens, 'hid', axis=0, tiled=True)  105 us
    all_gather x1, waiting for transfers between devices, local(): piece = lax.all_gather(cotangent, 'hid', axis=0, tiled=True)  92.3 us
    all_gather x1, waiting for transfers between devices, gather_and_add(): parts = lax.all_gather(array, name, axis=0, tiled=False)  78.6 us
  transfers between devices with their start and end apart: 5, of which 5 were waited for; matrix products, arithmetic and copies ran while one was open for 2% of the time, Pallas kernels for 0%

profile of v2, /device:TPU:32, one launch (start us, length us, event | category | flops | bytes accessed | tf_op | source)
XLA Modules:
  0.0 1002.9 jit_solution(9768891489685259752)
XLA Ops:
  7.2 0.0 all-gather.7.cloned.1.call-start
  7.2 0.7 all-gather.7.cloned.1.call-update
  7.9 0.0 all-gather.5.cloned.1.call-start
  8.0 0.7 all-gather.5.cloned.1.call-update
  8.7 0.0 all-gather.9.cloned.1.call-start
  8.7 104.6 %all-gather.7.cloned.1.call-done = bf16[512,1024]{1,0:T(8,128)(2,1)} async-done(((bf16[8,1024]{1,0:T(8,128)(2,1)}), bf16[512,1024]{1,0:T(8,128)(2,1)}) %all-gather.7.cloned.1.call-update) | async-done | bytes 1048592 | tf_op jit(solution)/shard_map/all_gather | solution.py:38
  113.3 3.0 convolution_convert_fusion.3
  116.2 0.0 all-gather.9.cloned.1.call-update
  116.3 0.0 all-reduce.3.cloned.1.call-start
  116.3 1.4 convolution_convert_fusion.2
  117.7 92.3 %all-gather.5.cloned.1.call-done = bf16[512,1024]{1,0:T(8,128)(2,1)} async-done(((bf16[8,1024]{1,0:T(8,128)(2,1)}), bf16[512,1024]{1,0:T(8,128)(2,1)}) %all-gather.5.cloned.1.call-update) | async-done | bytes 1048592 | tf_op jit(solution)/shard_map/all_gather | solution.py:42
  210.1 2.6 convolution_convert_fusion.4
  212.7 0.0 reduce-scatter.2.cloned.1.call-start
  212.8 78.6 %all-gather.9.cloned.1.call-done = bf16[4096,416]{0,1:T(8,128)(2,1)} async-done(((bf16[512,416]{0,1:T(8,128)(2,1)}), bf16[4096,416]{0,1:T(8,128)(2,1)}) %all-gather.9.cloned.1.call-update) | async-done | bytes 3407888 | tf_op jit(solution)/shard_map/all_gather | solution.py:10
  291.4 3.8 copy.9
  295.1 2.5 bitcast_reduce_fusion
  297.6 117.3 %all-reduce.3.cloned.1.call-done = (bf16[512,416]{0,1:T(8,128)(2,1)}, bf16[512,416]{0,1:T(8,128)(2,1)}) async-done(((bf16[512,416]{0,1:T(8,128)(2,1)}, bf16[512,416]{0,1:T(8,128)(2,1)}), (bf16[512,416]{0,1:T(8,128)(2,1)}, bf16[512,416]{0,1:T(8,128)(2,1)})) %all-reduce.3.cloned.1.call-update) | async-done | bytes 851984 | tf_op jit(solution)/shard_map/psum | solution.py:45
  415.0 2.2 fusion.13
  417.2 2.2 convolution_add_fusion
  419.4 1.6 fusion.1
  421.0 1.6 multiply_convert_fusion
  422.6 1.7 fusion
  424.4 570.6 %reduce-scatter.2.cloned.1.call-done = f32[8,1024]{1,0:T(8,128)} async-done(((f32[512,1024]{1,0:T(8,128)}), f32[8,1024]{1,0:T(8,128)}) %reduce-scatter.2.cloned.1.call-update) | async-done | bytes 32784 | tf_op jit(solution)/shard_map/reduce_scatter | solution.py:53
  995.0 1.4 convert_element_type.55
  (16 shorter events, 0.1 us)
Async XLA Ops:
  7.2 109.2 %copy-start = (bf16[1024,416]{0,1:T(8,128)(2,1)S(1)}, bf16[1024,416]{0,1:T(8,128)(2,1)}, u32[]{:S(2)}) copy-start(bf16[1024,416]{0,1:T(8,128)(2,1)} %param.7) | copy-start | bytes 2555908
  7.2 106.1 %all-gather.7.cloned.1.call-start = ((), (), s32[]{:S(2)}) async-start(), calls=%async_computation.2 | async-start | bytes 1064960 | tf_op jit(solution)/shard_map/all_gather | solution.py:38
  7.9 202.2 %all-gather.5.cloned.1.call-start = ((), (), s32[]{:S(2)}) async-start(), calls=%async_computation.1 | async-start | bytes 1064960 | tf_op jit(solution)/shard_map/all_gather | solution.py:42
  8.7 282.7 %all-gather.9.cloned.1.call-start = ((), (), s32[]{:S(2)}) async-start(), calls=%async_computation.4 | async-start | bytes 3833856 | tf_op jit(solution)/shard_map/all_gather | solution.py:10
  113.3 3.0 copy-start.1
  116.2 93.8 %copy-start.3 = (bf16[416,1024]{1,0:T(8,128)(2,1)S(1)}, bf16[416,1024]{1,0:T(8,128)(2,1)}, u32[]{:S(2)}) copy-start(bf16[416,1024]{1,0:T(8,128)(2,1)} %param.9) | copy-start | bytes 2555908
  116.3 298.7 %all-reduce.3.cloned.1.call-start = ((), (), s32[]{:S(2)}) async-start(), calls=%async_computation.5 | async-start | bytes 1703936 | tf_op jit(solution)/shard_map/psum | solution.py:45
  212.7 782.3 %reduce-scatter.2.cloned.1.call-start = ((), (), s32[]{:S(2)}) async-start(), calls=%async_computation.3 | async-start | bytes 2129920 | tf_op jit(solution)/shard_map/reduce_scatter | solution.py:53
  415.0 2.2 copy-start.4
  415.0 2.2 copy-start.5
  415.0 2.2 copy-start.6
  419.4 1.6 copy-start.2
Sparse Core Ops, SparseCore 0:
  12.4 100.8 all-gather.6
  117.6 92.4 all-gather.4
  212.7 78.5 all-gather.8
  294.8 120.1 all-reduce.2
  419.5 575.4 reduce-scatter.1
